TPU v7x, 32 devices: a whole 2x2x4 slice. The times are simulated.
32 devices in a mesh: job: 2 (over x), actor: 8 (over z, y), tp: 2 (over core).
Axes of the slice: x: 2, y: 2, z: 4, core: 2. Of those that a mesh axis runs over, the one named last changes fastest.
Arguments:
- leaf_states: bfloat16 [4096, 5120], P(('job', 'actor')), parts along dimension 0, may hold values from -6 to 6
- norm_gain: bfloat16 [5120], replicated, may hold values from 0.25 to 1.75
- wq_quant: bfloat16 [5120, 2560], P('actor', 'tp'), may hold values from -4 to 4
- wq_scale: float32 [40, 20], P(None, 'tp'), may hold values from 0.0069877123 to 0.02795085
- key_weight_quantized: bfloat16 [5120, 512], P('actor', 'tp'), may hold values from -4 to 4
- key_weight_scale: float32 [40, 4], P(None, 'tp'), may hold values from 0.0069877123 to 0.02795085
- value_weight_quantized: bfloat16 [5120, 512], P('actor', 'tp'), may hold values from -4 to 4
- value_weight_scale: float32 [40, 4], P(None, 'tp'), may hold values from 0.0069877123 to 0.02795085
- wo_quant: bfloat16 [2560, 5120], P('tp', 'actor'), may hold values from -4 to 4
- wo_scale: float32 [20, 40], P('tp'), may hold values from 0.019764235 to 0.07905694
- q_bias: bfloat16 [2560], P('tp'), may hold values from -2 to 2
- key_bias: bfloat16 [512], P('tp'), may hold values from -2 to 2
- value_bias: bfloat16 [512], P('tp'), may hold values from -3 to 3
- prefix_key_cache: bfloat16 [32, 2048, 512], P(('job', 'actor'), None, 'tp'), parts along dimension 0, may hold values from -140 to 140
- prefix_value_cache: bfloat16 [32, 2048, 512], P(('job', 'actor'), None, 'tp'), parts along dimension 0, may hold values from -15 to 15
- parent_prefix_slot: int32 [4096], P(('job', 'actor')), parts along dimension 0, may hold values from 0 to 1
- prefix_length: int32 [4096], P(('job', 'actor')), parts along dimension 0, may hold values from 1 to 2048, as said below
Outputs:
- attn_out: bfloat16 [4096, 5120], P(('job', 'actor')), parts along dimension 0
There are 2 independent parts, one for each index of `job`. A program takes and returns all parts, laid end to end along the dimension named above; an argument that names none is the same for every part. Nothing has to cross between parts.
Inputs may be any that keep to these rules, and one draw needn't show every extreme that they name: parent_prefix_slot numbers the leaf's prefix among the 2 prefixes of its own actor replica's block of the cache (leaf t belongs to replica t // 256, whose prefixes are cache rows 2 r to 2 r + 1). `prefix_length`: the first leaf of every actor replica sees all 2048 cached positions.
All inputs are finite; a program needn't handle non-finite values.
Results may differ from a plain program's by a relative error of at most 0.0045.
The roundings to bfloat16 on the way count: a program that leaves them out, or rounds other values in their place, can miss the bound.
Values may be sent and summed in bfloat16 or wider, within the bound.
A program may use at most 192 MiB of HBM per device.

v0:
```python
import math

import jax
import jax.numpy as jnp
from jax import lax
from jax.sharding import PartitionSpec as P

HEAD_WIDTH = 128
SCALE_BLOCK = 128


epsilon = 1e-06
rope_base = 1000000.0


def apply_rotary(values, length):
    width = values.shape[-1]
    half_width = width // 2
    freqs = rope_base ** (-(jnp.arange(half_width, dtype=jnp.float32) * 2.0 / width))
    angles = length.astype(jnp.float32)[:, None] * freqs[None, :]
    cosine = jnp.cos(angles)[:, None, :]
    sine = jnp.sin(angles)[:, None, :]
    first = values[..., :half_width]
    second = values[..., half_width:]
    return jnp.concatenate(
        [first * cosine - second * sine, second * cosine + first * sine], axis=-1
    )


def attend_single_head(
    query_vector, key_self, value_self, prefix_key_cache, prefix_value_cache, parent, length
):
    scale_factor = 1.0 / math.sqrt(query_vector.shape[-1])
    self_score = (
        jnp.sum(
            query_vector.astype(jnp.float32) * key_self.astype(jnp.float32)[:, None, :], axis=-1
        )
        * scale_factor
    )
    visible = (jnp.arange(prefix_key_cache.shape[1])[None, :] < length[:, None])[:, None, :]
    outcome = jnp.zeros(query_vector.shape, jnp.float32)
    for prefix_index in range(prefix_key_cache.shape[0]):
        scores = (
            jnp.einsum(
                "lge,ce->lgc",
                query_vector,
                prefix_key_cache[prefix_index],
                preferred_element_type=jnp.float32,
            )
            * scale_factor
        )
        highest = jnp.maximum(jnp.max(jnp.where(visible, scores, -jnp.inf), axis=-1), self_score)
        weights = jnp.where(visible, jnp.exp(scores - highest[..., None]), 0.0)
        self_weight = jnp.exp(self_score - highest)
        total = jnp.sum(weights, axis=-1) + self_weight
        self_rounded = lax.optimization_barrier(self_weight.astype(jnp.bfloat16)).astype(
            jnp.float32
        )
        mixed = jnp.einsum(
            "lgc,ce->lge",
            weights.astype(jnp.bfloat16),
            prefix_value_cache[prefix_index],
            preferred_element_type=jnp.float32,
        )
        mixed = mixed + self_rounded[..., None] * value_self.astype(jnp.float32)[:, None, :]
        outcome = jnp.where(
            (parent == prefix_index)[:, None, None], mixed / total[..., None], outcome
        )
    return outcome


def per_device(
    leaf_states,
    norm_gain,
    wq_quant,
    wq_scale,
    key_weight_quantized,
    key_weight_scale,
    value_weight_quantized,
    value_weight_scale,
    wo_quant,
    wo_scale,
    q_bias,
    key_bias,
    value_bias,
    prefix_key_cache,
    prefix_value_cache,
    parent_prefix_slot,
    prefix_length,
):
    states = leaf_states.astype(jnp.float32)
    normed = (
        states
        * lax.rsqrt(jnp.mean(states * states, axis=-1, keepdims=True) + epsilon)
        * norm_gain.astype(jnp.float32)
    ).astype(jnp.bfloat16)
    leaf_count = normed.shape[0]
    row_count = wq_quant.shape[0]
    row_start = lax.axis_index("actor") * row_count

    def expand_rows(quant, scale):
        tall = jnp.repeat(scale, SCALE_BLOCK, axis=0)
        mine = lax.dynamic_slice_in_dim(tall, row_start, row_count, 0)
        return (quant.astype(jnp.float32) * jnp.repeat(mine, SCALE_BLOCK, axis=1)).astype(
            jnp.bfloat16
        )

    wq_local = expand_rows(wq_quant, wq_scale)
    wk_local = expand_rows(key_weight_quantized, key_weight_scale)
    wv_local = expand_rows(value_weight_quantized, value_weight_scale)
    pieces = (
        lax.all_gather(wq_local, "actor", axis=0, tiled=True),
        lax.all_gather(wk_local, "actor", axis=0, tiled=True),
        lax.all_gather(wv_local, "actor", axis=0, tiled=True),
    )
    query_sum, key_sum, value_sum = tuple(
        (jnp.dot(normed, piece, preferred_element_type=jnp.float32) for piece in pieces)
    )
    heads_local = query_sum.shape[1] // HEAD_WIDTH
    kv_local = key_sum.shape[1] // HEAD_WIDTH
    query_group = heads_local // kv_local
    query_vector = apply_rotary(
        (query_sum + q_bias.astype(jnp.float32)).reshape(leaf_count, heads_local, HEAD_WIDTH),
        prefix_length,
    ).astype(jnp.bfloat16)
    query_vector = query_vector.reshape(leaf_count, kv_local, query_group, HEAD_WIDTH)
    fresh_key = apply_rotary(
        (key_sum + key_bias.astype(jnp.float32)).reshape(leaf_count, kv_local, HEAD_WIDTH),
        prefix_length,
    ).astype(jnp.bfloat16)
    fresh_value = (
        (value_sum + value_bias.astype(jnp.float32))
        .reshape(leaf_count, kv_local, HEAD_WIDTH)
        .astype(jnp.bfloat16)
    )
    head_list = []
    for head_number in range(kv_local):
        lower = head_number * HEAD_WIDTH
        upper = lower + HEAD_WIDTH
        head_list.append(
            attend_single_head(
                query_vector[:, head_number],
                fresh_key[:, head_number],
                fresh_value[:, head_number],
                prefix_key_cache[:, :, lower:upper],
                prefix_value_cache[:, :, lower:upper],
                parent_prefix_slot,
                prefix_length,
            )
        )
    attended = (
        jnp.stack(head_list, axis=1)
        .reshape(leaf_count, heads_local * HEAD_WIDTH)
        .astype(jnp.bfloat16)
    )
    col_count = wo_quant.shape[1]
    col_start = lax.axis_index("actor") * col_count
    spread_scale = jnp.repeat(wo_scale, SCALE_BLOCK, axis=1)
    own_scale = lax.dynamic_slice_in_dim(spread_scale, col_start, col_count, 1)
    wo_local = (wo_quant.astype(jnp.float32) * jnp.repeat(own_scale, SCALE_BLOCK, axis=0)).astype(
        jnp.bfloat16
    )
    partial_out = jnp.dot(
        attended,
        lax.all_gather(wo_local, "actor", axis=1, tiled=True),
        preferred_element_type=jnp.float32,
    )
    return lax.psum(partial_out, "tp").astype(jnp.bfloat16)


def solution(mesh):
    placed = (
        P(("job", "actor"), None),
        P(),
        P("actor", "tp"),
        P(None, "tp"),
        P("actor", "tp"),
        P(None, "tp"),
        P("actor", "tp"),
        P(None, "tp"),
        P("tp", "actor"),
        P("tp", None),
        P("tp"),
        P("tp"),
        P("tp"),
        P(("job", "actor"), None, "tp"),
        P(("job", "actor"), None, "tp"),
        P(("job", "actor")),
        P(("job", "actor")),
    )
    return jax.shard_map(
        per_device, mesh=mesh, in_specs=placed, out_specs=P(("job", "actor"), None), check_vma=False
    )
```

profile of v0, /device:TPU:0, one launch (start us, length us, event | category | flops | bytes accessed | tf_op | source)
XLA Modules:
  0.0 524.4 jit_solution(13400303724975240623)
XLA Ops:
  6.6 0.8 copy.39
  7.4 0.8 copy.33
  8.6 0.8 broadcast_in_dim.132
  9.4 0.8 fusion.75
  10.3 0.8 broadcast_in_dim.135
  11.2 0.8 fusion.74
  12.2 0.8 copy.49
  13.0 1.3 copy.29
  14.3 0.8 constant_dynamic-slice_fusion.3
  15.1 1.5 fusion.24
  17.0 3.1 fusion.23
  22.3 45.5 %all-gather.7.cloned.1.call-done = bf16[5120,256]{1,0:T(8,128)(2,1)} async-done(((bf16[640,256]{1,0:T(8,128)(2,1)}), bf16[5120,256]{1,0:T(8,128)(2,1)}) %all-gather.7.cloned.1.call-update) | async-done | bytes 2621456 | tf_op jit(solution)/shard_map/all_gather | solution.py:113
  67.8 3.9 convolution_add_fusion.2
  72.2 51.0 %all-gather.9.cloned.1.call-done = bf16[5120,256]{1,0:T(8,128)(2,1)} async-done(((bf16[640,256]{1,0:T(8,128)(2,1)}), bf16[5120,256]{1,0:T(8,128)(2,1)}) %all-gather.9.cloned.1.call-update) | async-done | bytes 2621456 | tf_op jit(solution)/shard_map/all_gather | solution.py:114
  123.2 4.0 fusion.37
  127.2 0.7 fusion.105
  127.9 179.0 %all-gather.5.cloned.1.call-done = bf16[5120,1280]{0,1:T(8,128)(2,1)} async-done(((bf16[640,1280]{0,1:T(8,128)(2,1)}), bf16[5120,1280]{0,1:T(8,128)(2,1)}) %all-gather.5.cloned.1.call-update) | async-done | bytes 13107216 | tf_op jit(solution)/shard_map/all_gather | solution.py:112
  306.9 8.2 %convolution_add_fusion = f32[256,1280]{1,0:T(8,128)S(1)} fusion(bf16[5120,1280]{0,1:T(8,128)(2,1)} %all-gather.5.cloned.1.call-done, f32[1280]{0:T(1024)S(1)} %convert_element_type.119, bf16[256,5120]{1,0:T(8,128)(2,1)} %param.17, f32[5120]{0:T(1024)S(1)} %copy-done.12, f32[256]{0:T(256)S(1)} %add_rsqrt_fusion), kind=kOutput, calls=%fused_computation.33 | convolution fusion | flops 3361013760 | bytes 17065984 | tf_op jit(solution)/shard_map/dot_general | solution.py:117
  316.4 0.8 multiply_reduce_fusion.1
  317.2 2.8 fusion.86
  320.0 6.5 %select_reduce_fusion.2 = (f32[256,5]{0,1:T(8,128)S(1)}, f32[256,5]{0,1:T(8,128)S(1)}, f32[256,5,2048]{2,0,1:T(8,128)}) fusion(pred[256,2048]{1,0:T(8,128)(4,1)S(1)} %iota_compare_fusion, f32[256,5,2048]{2,0,1:T(8,128)S(1)} %fusion.86, bf16[256,5,128]{2,0,1:T(8,128)(2,1)S(1)} %get-tuple-element.16, bf16[2,2048,256]{2,1,0:T(8,128)(2,1)S(1)} %copy-done.6), kind=kOutput, calls=%fused_computation.5 | convolution fusion | flops 686814720 | bytes 22358016 | tf_op jit(solution)/shard_map/lge,ce->lgc/dot_general | solution.py:44
  326.5 0.6 copy-done.2
  327.1 5.4 %fusion.80 = f32[256,5,2048]{2,0,1:T(8,128)} fusion(bf16[256,5,128]{2,0,1:T(8,128)(2,1)S(1)} %get-tuple-element.20, bf16[2,2048,256]{2,1,0:T(8,128)(2,1)S(1)} %copy-done.6), kind=kOutput, calls=%fused_computation.69 | convolution fusion | flops 671088640 | bytes 11337728 | tf_op jit(solution)/shard_map/lge,ce->lgc/dot_general | solution.py:44
  332.6 16.4 %fusion.2 = (f32[256,5]{0,1:T(8,128)S(1)}, f32[256,5]{0,1:T(8,128)S(1)}, f32[256,5]{0,1:T(8,128)S(1)}, f32[256,5]{0,1:T(8,128)S(1)}, f32[256,5,2048]{2,0,1:T(8,128)}) fusion(f32[256,5,2048]{2,0,1:T(8,128)} %get-tuple-element.49, f32[256,5]{0,1:T(8,128)S(1)} %get-tuple-element.44, pred[256,2048]{1,0:T(8,128)(4,1)S(1)} %iota_compare_fusion, ...), kind=kOutput, calls=%fused_computation.10 | convolution fusion | flops 707783680 | bytes 43356160 | tf_op jit(solution)/shard_map/lge,ce->lgc/dot_general | solution.py:44
  349.0 10.8 %fusion.6 = (f32[256,5]{0,1:T(8,128)S(1)}, f32[256,5]{0,1:T(8,128)S(1)}) fusion(f32[256,5,2048]{2,0,1:T(8,128)} %fusion.80, f32[256,5]{0,1:T(8,128)S(1)} %get-tuple-element.41, pred[256,2048]{1,0:T(8,128)(4,1)S(1)} %iota_compare_fusion, f32[256,5]{0,1:T(8,128)S(1)} %get-tuple-element.42, f32[256,5,2048]{2,0,1:T(8,128)} %get-tuple-element.50), kind=kLoop, calls=%fused_computation.14 | loop fusion | flops 20968960 | bytes 21516288 | tf_op jit(solution)/shard_map/reduce_sum | solution.py:55
  360.0 2.7 fusion.71
  362.7 6.7 %fusion.53 = bf16[256,5,128]{0,2,1:T(8,128)(2,1)S(1)} fusion(f32[256,5,2048]{2,0,1:T(8,128)} %get-tuple-element.50, f32[256,5]{0,1:T(8,128)S(1)} %get-tuple-element.42, pred[256,2048]{1,0:T(8,128)(4,1)S(1)} %iota_compare_fusion, bf16[2,2048,256]{2,1,0:T(8,128)(2,1)S(1)} %copy-done.18, f32[256,5]{0,1:T(8,128)S(1)} %get-tuple-element.39, ...), kind=kOutput, calls=%fused_computation.47 | convolution fusion | flops 682229760 | bytes 12017664 | tf_op jit(solution)/shard_map/lgc,ce->lge/dot_general | solution.py:59
  369.4 2.7 fusion.68
  372.2 2.7 fusion.50
  375.0 115.0 %all-gather.11.cloned.1.call-done = bf16[1280,5120]{1,0:T(8,128)(2,1)} async-done(((bf16[1280,640]{1,0:T(8,128)(2,1)}), bf16[1280,5120]{1,0:T(8,128)(2,1)}) %all-gather.11.cloned.1.call-update) | async-done | bytes 13107216 | tf_op jit(solution)/shard_map/all_gather | solution.py:165
  490.0 10.1 %fusion.128 = f32[256,5120]{1,0:T(8,128)} fusion(bf16[256,1280]{0,1:T(8,128)(2,1)S(1)} %bitcast.121, bf16[1280,5120]{1,0:T(8,128)(2,1)} %all-gather.11.cloned.1.call-done), kind=kOutput, calls=%fused_computation.139 | convolution fusion | flops 3355443200 | bytes 19005440 | tf_op jit(solution)/shard_map/dot_general | solution.py:163
  500.2 17.7 %all-reduce.1 = bf16[256,5120]{1,0:T(8,128)(2,1)} all-reduce(f32[256,5120]{1,0:T(8,128)} %fusion.128), channel_id=1, replica_groups=mesh['job'=2,'actor'=8,'tp'=2] {'tp'}, use_global_device_ids=true, to_apply=%region_11.12 | all-reduce | flops 1310720 | bytes 7864320 | tf_op jit(solution)/shard_map/psum | solution.py:168
  (105 shorter events, 5.0 us)
Async XLA Ops:
  6.5 5.5 %copy-start = (f32[40,10]{0,1:T(8,128)S(1)}, f32[40,10]{0,1:T(8,128)}, u32[]{:S(2)}) copy-start(f32[40,10]{0,1:T(8,128)} %param.20) | copy-start | bytes 4804
  6.5 2.9 copy-start.7
  6.5 4.6 copy-start.8
  6.5 61.2 %all-gather.7.cloned.1.call-start = ((), (), s32[]{:S(2)}) async-start(), calls=%async_computation.1 | async-start | bytes 2949120 | tf_op jit(solution)/shard_map/all_gather | solution.py:113
  8.3 4.7 copy-start.5
  10.3 113.0 %all-gather.9.cloned.1.call-start = ((), (), s32[]{:S(2)}) async-start(), calls=%async_computation.2 | async-start | bytes 2949120 | tf_op jit(solution)/shard_map/all_gather | solution.py:114
  12.0 4.7 copy-start.14
  12.0 294.9 %all-gather.5.cloned.1.call-start = ((), (), s32[]{:S(2)}) async-start(), calls=%async_computation | async-start | bytes 14745600 | tf_op jit(solution)/shard_map/all_gather | solution.py:112
  15.1 5.0 copy-start.13
  15.1 5.0 copy-start.19
  15.1 5.0 copy-start.15
  15.1 5.5 %copy-start.16 = (bf16[1280]{0:T(1024)(128)(2,1)S(1)}, bf16[1280]{0:T(1024)(128)(2,1)}, u32[]{:S(2)}) copy-start(bf16[1280]{0:T(1024)(128)(2,1)} %param.27) | copy-start | bytes 7684
  15.1 5.6 %copy-start.20 = (bf16[256]{0:T(256)(128)(2,1)S(1)}, bf16[256]{0:T(256)(128)(2,1)}, u32[]{:S(2)}) copy-start(bf16[256]{0:T(256)(128)(2,1)} %param.29) | copy-start | bytes 1540
  16.6 4.6 copy-start.4
  16.6 5.2 %copy-start.17 = (s32[256]{0:T(256)S(1)}, s32[256]{0:T(256)}, u32[]{:S(2)}) copy-start(s32[256]{0:T(256)} %param.32) | copy-start | bytes 3076
  16.7 473.4 %all-gather.11.cloned.1.call-start = ((), (), s32[]{:S(2)}) async-start(), calls=%async_computation.3 | async-start | bytes 14745600 | tf_op jit(solution)/shard_map/all_gather | solution.py:165
  20.1 51.6 %copy-start.11 = (f32[5120]{0:T(1024)}, f32[5120]{0:T(1024)S(1)}, u32[]{:S(2)}) copy-start(f32[5120]{0:T(1024)S(1)} %convert_element_type.115) | copy-start | bytes 61444
  22.3 100.9 %copy-start.21 = (f32[256]{0:T(256)S(1)}, f32[256]{0:T(256)}, u32[]{:S(2)}) copy-start(f32[256]{0:T(256)} %convert_element_type.130) | copy-start | bytes 3076
  71.7 235.2 %copy-start.12 = (f32[5120]{0:T(1024)S(1)}, f32[5120]{0:T(1024)}, u32[]{:S(2)}) copy-start(f32[5120]{0:T(1024)} %copy-done.11) | copy-start | bytes 61444
  317.1 2.9 copy-start.6
  320.0 7.1 %copy-start.2 = (f32[256,5,2048]{2,0,1:T(8,128)}, f32[256,5,2048]{2,0,1:T(8,128)S(1)}, u32[]{:S(2)}) copy-start(f32[256,5,2048]{2,0,1:T(8,128)S(1)} %fusion.86) | copy-start | bytes 31457284
  349.0 10.9 %copy-start.3 = (f32[256,5,2048]{2,0,1:T(8,128)S(1)}, f32[256,5,2048]{2,0,1:T(8,128)}, u32[]{:S(2)}) copy-start(f32[256,5,2048]{2,0,1:T(8,128)} %copy-done.2) | copy-start | bytes 31457284
  349.0 10.9 %copy-start.10 = (f32[256,128]{0,1:T(8,128)S(1)}, f32[256,128]{0,1:T(8,128)}, u32[]{:S(2)}) copy-start(f32[256,128]{0,1:T(8,128)} %get-tuple-element.27) | copy-start | bytes 393220
  349.0 10.9 %copy-start.18 = (bf16[2,2048,256]{2,1,0:T(8,128)(2,1)S(1)}, bf16[2,2048,256]{2,1,0:T(8,128)(2,1)}, u32[]{:S(2)}) copy-start(bf16[2,2048,256]{2,1,0:T(8,128)(2,1)} %param.31) | copy-start | bytes 6291460
  359.9 2.7 copy-start.9
  360.0 9.4 %slice-start.3 = ((s8[10485760]{0:T(1024)(128)(4,1)}), s8[4194304]{0:T(1024)(128)(4,1)S(1)}, s32[]{:S(2)}) async-start(s8[10485760]{0:T(1024)(128)(4,1)} %bitcast.116), calls=%async_computation.7 | async-start | bytes 8388608
  360.0 9.4 %slice-start.4 = ((s8[10485760]{0:T(1024)(128)(4,1)}), s8[4194304]{0:T(1024)(128)(4,1)S(1)}, s32[]{:S(2)}) async-start(s8[10485760]{0:T(1024)(128)(4,1)} %bitcast.116), calls=%async_computation.8 | async-start | bytes 8388608
  362.7 6.7 %slice-start.5 = ((s8[10485760]{0:T(1024)(128)(4,1)}), s8[2097152]{0:T(1024)(128)(4,1)S(1)}, s32[]{:S(2)}) async-start(s8[10485760]{0:T(1024)(128)(4,1)} %bitcast.116), calls=%async_computation.9 | async-start | bytes 4194304
  362.7 9.5 %slice-start = ((s8[10485760]{0:T(1024)(128)(4,1)}), s8[4194304]{0:T(1024)(128)(4,1)S(1)}, s32[]{:S(2)}) async-start(s8[10485760]{0:T(1024)(128)(4,1)} %bitcast.114), calls=%async_computation.4 | async-start | bytes 8388608
  362.7 9.5 %slice-start.1 = ((s8[10485760]{0:T(1024)(128)(4,1)}), s8[4194304]{0:T(1024)(128)(4,1)S(1)}, s32[]{:S(2)}) async-start(s8[10485760]{0:T(1024)(128)(4,1)} %bitcast.114), calls=%async_computation.5 | async-start | bytes 8388608
  369.4 2.8 slice-start.2
  490.0 27.8 %copy-start.1 = (f32[40,10]{0,1:T(8,128)S(1)}, f32[40,10]{0,1:T(8,128)}, u32[]{:S(2)}) copy-start(f32[40,10]{0,1:T(8,128)} %param.20) | copy-start | bytes 4804
Sparse Core Ops, SparseCore 0:
  10.4 57.3 all-gather.6
  70.0 53.2 all-gather.8
  125.5 181.3 all-gather.4
  309.0 181.0 all-gather.10
where the time goes:
time: 525 us; the launch traced here: 524 us
  waiting for transfers between devices  391 us (74%)
  matrix products  72.2 us (14%)
  other arithmetic  20.9 us (4%)
  blocking collectives  17.7 us (3%)
  between operations  13.8 us (3%)
  local copies, waits for them, and re-layouts  9.09 us (2%)
    all_gather x1, waiting for transfers between devices, per_device(): lax.all_gather(wq_local, 'actor', axis=0, tiled=True)  179 us
    all_gather x1, waiting for transfers between devices, per_device(): lax.all_gather(wo_local, 'actor', axis=1, tiled=True)  115 us
    all_gather x1, waiting for transfers between devices, per_device(): lax.all_gather(wv_local, 'actor', axis=0, tiled=True)  51 us
    all_gather x1, waiting for transfers between devices, per_device(): lax.all_gather(wk_local, 'actor', axis=0, tiled=True)  45.5 us
    dot_general x4, matrix products, attend_single_head(): jnp.einsum('lge,ce->lgc', query_vector, prefix_key_cache[prefix_index], p...  31.2 us
    psum x1, blocking collectives, per_device(): return lax.psum(partial_out, 'tp').astype(jnp.bfloat16)  17.7 us
    dot_general x3, matrix products, per_device(): jnp.dot(normed, piece, preferred_element_type=jnp.float32)  16 us
    dot_general x4, matrix products, attend_single_head(): jnp.einsum('lgc,ce->lge', weights.astype(jnp.bfloat16), prefix_value_cach...  14.8 us
  transfers between devices with their start and end apart: 4, of which 4 were waited for; matrix products, arithmetic and copies ran while one was open for 17% of the time, Pallas kernels for 0%

commit v1 on v0

v1 whole, which is shorter than its diff:
```python
import functools
import math

import jax
import jax.numpy as jnp
from jax import lax
from jax.sharding import PartitionSpec as P

HEAD_WIDTH = 128
SCALE_BLOCK = 128


epsilon = 1e-06
rope_base = 1000000.0


def apply_rotary(values, length):
    width = values.shape[-1]
    half_width = width // 2
    freqs = rope_base ** (-(jnp.arange(half_width, dtype=jnp.float32) * 2.0 / width))
    angles = length.astype(jnp.float32)[:, None] * freqs[None, :]
    cosine = jnp.cos(angles)[:, None, :]
    sine = jnp.sin(angles)[:, None, :]
    first = values[..., :half_width]
    second = values[..., half_width:]
    return jnp.concatenate(
        [first * cosine - second * sine, second * cosine + first * sine], axis=-1
    )


def attend_single_head(
    query_vector, key_self, value_self, prefix_key_cache, prefix_value_cache, parent, length
):
    scale_factor = 1.0 / math.sqrt(query_vector.shape[-1])
    self_score = (
        jnp.sum(
            query_vector.astype(jnp.float32) * key_self.astype(jnp.float32)[:, None, :], axis=-1
        )
        * scale_factor
    )
    visible = (jnp.arange(prefix_key_cache.shape[1])[None, :] < length[:, None])[:, None, :]
    outcome = jnp.zeros(query_vector.shape, jnp.float32)
    for prefix_index in range(prefix_key_cache.shape[0]):
        scores = (
            jnp.einsum(
                "lge,ce->lgc",
                query_vector,
                prefix_key_cache[prefix_index],
                preferred_element_type=jnp.float32,
            )
            * scale_factor
        )
        highest = jnp.maximum(jnp.max(jnp.where(visible, scores, -jnp.inf), axis=-1), self_score)
        weights = jnp.where(visible, jnp.exp(scores - highest[..., None]), 0.0)
        self_weight = jnp.exp(self_score - highest)
        total = jnp.sum(weights, axis=-1) + self_weight
        self_rounded = lax.optimization_barrier(self_weight.astype(jnp.bfloat16)).astype(
            jnp.float32
        )
        mixed = jnp.einsum(
            "lgc,ce->lge",
            weights.astype(jnp.bfloat16),
            prefix_value_cache[prefix_index],
            preferred_element_type=jnp.float32,
        )
        mixed = mixed + self_rounded[..., None] * value_self.astype(jnp.float32)[:, None, :]
        outcome = jnp.where(
            (parent == prefix_index)[:, None, None], mixed / total[..., None], outcome
        )
    return outcome


def per_device(
    mesh_sizes,
    leaf_states,
    norm_gain,
    wq_quant,
    wq_scale,
    key_weight_quantized,
    key_weight_scale,
    value_weight_quantized,
    value_weight_scale,
    wo_quant,
    wo_scale,
    q_bias,
    key_bias,
    value_bias,
    prefix_key_cache,
    prefix_value_cache,
    parent_prefix_slot,
    prefix_length,
):
    n_job, n_actor = mesh_sizes
    swap = [(i, i ^ 1) for i in range(n_job)]
    side = lax.axis_index("job") % 2
    actor = lax.axis_index("actor")

    def trade(x):
        return lax.ppermute(x, "job", swap)

    states = leaf_states.astype(jnp.float32)
    normed = (
        states
        * lax.rsqrt(jnp.mean(states * states, axis=-1, keepdims=True) + epsilon)
        * norm_gain.astype(jnp.float32)
    ).astype(jnp.bfloat16)
    leaf_count = normed.shape[0]
    both_normed = jnp.concatenate([normed, trade(normed)], axis=0)
    both_length = jnp.concatenate([prefix_length, trade(prefix_length)], axis=0)

    def half_cols(x):
        width = x.shape[1] // 2
        return lax.dynamic_slice_in_dim(x, side * width, width, 1)

    row_count = wq_quant.shape[0]

    def expand_rows(quant, scale):
        mine = lax.dynamic_slice_in_dim(
            scale, actor * (row_count // SCALE_BLOCK), row_count // SCALE_BLOCK, 0
        ) if row_count % SCALE_BLOCK == 0 else None
        if mine is None:
            tall = jnp.repeat(scale, SCALE_BLOCK, axis=0)
            tall = lax.dynamic_slice_in_dim(tall, actor * row_count, row_count, 0)
        else:
            tall = jnp.repeat(mine, SCALE_BLOCK, axis=0)
        wide = jnp.repeat(half_cols(tall), SCALE_BLOCK, axis=1)
        return (half_cols(quant).astype(jnp.float32) * wide).astype(jnp.bfloat16)

    qkv_local = jnp.concatenate(
        [
            expand_rows(wq_quant, wq_scale),
            expand_rows(key_weight_quantized, key_weight_scale),
            expand_rows(value_weight_quantized, value_weight_scale),
        ],
        axis=1,
    )
    qkv_weight = lax.all_gather(qkv_local, "actor", axis=0, tiled=True)
    sums = jnp.dot(both_normed, qkv_weight, preferred_element_type=jnp.float32)

    def half_row(x):
        width = x.shape[0] // 2
        return lax.dynamic_slice_in_dim(x, side * width, width, 0)

    bias = jnp.concatenate([half_row(q_bias), half_row(key_bias), half_row(value_bias)])
    sums = sums + bias.astype(jnp.float32)
    v_width = value_bias.shape[0] // 2
    rot_width = sums.shape[1] - v_width
    rotated = apply_rotary(
        sums[:, :rot_width].reshape(2 * leaf_count, rot_width // HEAD_WIDTH, HEAD_WIDTH),
        both_length,
    ).reshape(2 * leaf_count, rot_width)
    done = jnp.concatenate([rotated, sums[:, rot_width:]], axis=1).astype(jnp.bfloat16)
    own = done[:leaf_count]
    other = trade(done[leaf_count:])
    q_width = q_bias.shape[0] // 2

    kv_half = v_width // HEAD_WIDTH
    query_group = q_bias.shape[0] // key_bias.shape[0]
    outs = []
    for which, block in ((side, own), (1 - side, other)):
        q = block[:, :q_width].reshape(leaf_count, kv_half, query_group, HEAD_WIDTH)
        k = block[:, q_width : q_width + v_width].reshape(leaf_count, kv_half, HEAD_WIDTH)
        v = block[:, q_width + v_width :].reshape(leaf_count, kv_half, HEAD_WIDTH)
        for head in range(kv_half):
            at = (which * kv_half + head) * HEAD_WIDTH
            outs.append(
                attend_single_head(
                    q[:, head],
                    k[:, head],
                    v[:, head],
                    lax.dynamic_slice_in_dim(prefix_key_cache, at, HEAD_WIDTH, 2),
                    lax.dynamic_slice_in_dim(prefix_value_cache, at, HEAD_WIDTH, 2),
                    parent_prefix_slot,
                    prefix_length,
                )
                .reshape(leaf_count, query_group * HEAD_WIDTH)
                .astype(jnp.bfloat16)
            )
    mine = jnp.concatenate(outs[:kv_half], axis=1)
    theirs = jnp.concatenate(outs[kv_half:], axis=1)
    attended = jnp.where(
        side == 0,
        jnp.concatenate([mine, theirs], axis=1),
        jnp.concatenate([theirs, mine], axis=1),
    )

    col_count = wo_quant.shape[1]
    spread_scale = jnp.repeat(wo_scale, SCALE_BLOCK, axis=1)
    own_scale = half_cols(lax.dynamic_slice_in_dim(spread_scale, actor * col_count, col_count, 1))
    wo_local = (
        half_cols(wo_quant).astype(jnp.float32) * jnp.repeat(own_scale, SCALE_BLOCK, axis=0)
    ).astype(jnp.bfloat16).T
    wo_all = lax.all_gather(wo_local, "actor", axis=0, tiled=True)
    both_attended = jnp.stack([attended, trade(attended)])
    group = lax.axis_index("tp")

    def project(rows):
        return lax.dot_general(
            rows, wo_all, (((1,), (1,)), ((), ())), preferred_element_type=jnp.float32
        )

    keep = project(lax.dynamic_index_in_dim(both_attended, group, 0, keepdims=False))
    give = project(lax.dynamic_index_in_dim(both_attended, 1 - group, 0, keepdims=False))
    got = lax.ppermute(give, "tp", [(0, 1), (1, 0)])
    total = (keep + got).astype(jnp.bfloat16)
    away = trade(total)
    local = jnp.where(group == 0, total, away)
    remote = lax.ppermute(local, "tp", [(0, 1), (1, 0)])
    mine_first = side == group
    low = jnp.where(mine_first, local, remote)
    high = jnp.where(mine_first, remote, local)
    pieces = []
    half = col_count // 2
    for a in range(n_actor):
        pieces += [low[:, a * half : (a + 1) * half], high[:, a * half : (a + 1) * half]]
    return jnp.concatenate(pieces, axis=1)


def solution(mesh):
    placed = (
        P(("job", "actor"), None),
        P(),
        P("actor", "tp"),
        P(None, "tp"),
        P("actor", "tp"),
        P(None, "tp"),
        P("actor", "tp"),
        P(None, "tp"),
        P("tp", "actor"),
        P("tp", None),
        P("tp"),
        P("tp"),
        P("tp"),
        P(("job", "actor"), None, "tp"),
        P(("job", "actor"), None, "tp"),
        P(("job", "actor")),
        P(("job", "actor")),
    )
    return jax.shard_map(
        functools.partial(per_device, (mesh.shape["job"], mesh.shape["actor"])),
        mesh=mesh,
        in_specs=placed,
        out_specs=P(("job", "actor"), None),
        check_vma=False,
    )
```

time: 525 us -> 328 us (0.62)
  waiting for transfers between devices: 391 us -> 178 us
  blocking collectives: 17.7 us -> 0 us
  local copies, waits for them, and re-layouts: 9.09 us -> 25 us
  starting transfers between devices: 0.13 us -> 8.43 us
  other arithmetic: 20.9 us -> 26.7 us
    all_gather x4 -> x2, waiting for transfers between devices: 391 us -> 87.6 us  [the longest x1 70.2 us: per_device(): qkv_weight = lax.all_gather(qkv_local, 'actor', axis=0, tiled=True)]
    ppermute x0 -> x7, waiting for transfers between devices: none -> 90.7 us  [the longest x5 82.8 us: trade(): return lax.ppermute(x, 'job', swap)]
    psum x1 -> x0, blocking collectives: 17.7 us -> none  [per_device(): return lax.psum(partial_out, 'tp').astype(jnp.bfloat16)]
    slice x1 -> x8, local copies, waits for them, and re-layouts: 0.02 us -> 8.86 us  [the longest x2 4.31 us: per_device(): sums[:, :rot_width]]
    ppermute x0 -> x7, starting transfers between devices: none -> 8.38 us  [the longest x5 7.48 us: trade(): return lax.ppermute(x, 'job', swap)]
    concatenate x0 -> x1, local copies, waits for them, and re-layouts: none -> 5.67 us  [per_device(): return jnp.concatenate(pieces, axis=1)]
    dot_general x4 -> x3, matrix products: 26.2 us -> 24.1 us  [the longest x2 12.4 us: project(): lax.dot_general(rows, wo_all, (((1,), (1,)), ((), ())), preferred_element...]
  transfers between devices with their start and end apart: 4 -> 9, of which waited for: 4 -> 7; matrix products, arithmetic and copies ran while one was open for 17% -> 28% of each run, Pallas kernels for 0% -> 0%
where the time goes in v1:
time: 328 us; the launch traced here: 323 us
  waiting for transfers between devices  178 us (54%)
  matrix products  70.6 us (22%)
  other arithmetic  26.7 us (8%)
  local copies, waits for them, and re-layouts  25 us (8%)
  between operations  14.3 us (4%)
  starting transfers between devices  8.43 us (3%)
    ppermute x5, waiting for transfers between devices, trade(): return lax.ppermute(x, 'job', swap)  82.8 us
    all_gather x1, waiting for transfers between devices, per_device(): qkv_weight = lax.all_gather(qkv_local, 'actor', axis=0, tiled=True)  70.2 us
    dot_general x4, matrix products, attend_single_head(): jnp.einsum('lge,ce->lgc', query_vector, prefix_key_cache[prefix_index], p...  31.8 us
    all_gather x1, waiting for transfers between devices, per_device(): wo_all = lax.all_gather(wo_local, 'actor', axis=0, tiled=True)  17.5 us
    dot_general x4, matrix products, attend_single_head(): jnp.einsum('lgc,ce->lge', weights.astype(jnp.bfloat16), prefix_value_cach...  14.7 us
    dot_general x2, matrix products, project(): lax.dot_general(rows, wo_all, (((1,), (1,)), ((), ())), preferred_element...  12.4 us
    dot_general x1, matrix products, per_device(): sums = jnp.dot(both_normed, qkv_weight, preferred_element_type=jnp.float32)  11.7 us
    reduce_sum x1, other arithmetic, attend_single_head(): total = jnp.sum(weights, axis=-1) + self_weight  10.8 us
  transfers between devices with their start and end apart: 9, of which 7 were waited for; matrix products, arithmetic and copies ran while one was open for 28% of the time, Pallas kernels for 0%

profile of v1, /device:TPU:0, one launch (start us, length us, event | category | flops | bytes accessed | tf_op | source)
XLA Modules:
  0.0 323.4 jit_solution(17247956283233276362)
XLA Ops:
  6.5 2.3 constant_dynamic-slice_fusion.9
  8.8 1.8 copy.80
  15.4 2.3 fusion.8
  17.8 4.0 %fusion.10 = bf16[256,5120]{1,0:T(8,128)(2,1)} fusion(bf16[256,5120]{1,0:T(8,128)(2,1)} %param.17, f32[5120]{0:T(1024)S(1)} %convert_element_type.138, f32[256]{0:T(256)S(1)} %add_rsqrt_fusion), kind=kLoop, calls=%fused_computation.20 | loop fusion | flops 5242880 | bytes 5264384 | tf_op jit(solution)/shard_map/convert_element_type | solution.py:106
  21.8 2.9 collective-permute-start
  25.1 2.0 fusion.28
  27.1 1.8 copy.75
  29.6 52.3 %collective-permute-done.1 = s32[256]{0:T(256)S(1)} collective-permute-done((s32[256]{0:T(256)S(1)}, s32[256]{0:T(256)S(1)}, u32[]{:S(2)}, u32[]{:S(2)}) %collective-permute-start.1) | collective-permute-done | bytes 1056 | tf_op jit(solution)/shard_map/ppermute | solution.py:99
  82.5 70.2 %all-gather.3.cloned.1.call-done = bf16[5120,896]{0,1:T(8,128)(2,1)} async-done(((bf16[640,896]{0,1:T(8,128)(2,1)}), bf16[5120,896]{0,1:T(8,128)(2,1)}) %all-gather.3.cloned.1.call-update) | async-done | bytes 9175056 | tf_op jit(solution)/shard_map/all_gather | solution.py:137
  152.7 11.7 %fusion.100 = (bf16[512,896]{1,0:T(8,128)(2,1)}, f32[512,896]{1,0:T(8,128)S(1)}) fusion(f32[896]{0:T(1024)S(1)} %maximum_convert_fusion, bf16[5120,896]{0,1:T(8,128)(2,1)} %all-gather.3.cloned.1.call-done, bf16[256,5120]{1,0:T(8,128)(2,1)} %collective-permute-done, bf16[256,5120]{1,0:T(8,128)(2,1)} %fusion.10), kind=kOutput, calls=%fused_computation.152 | convolution fusion | flops 4709023744 | bytes 17174016 | tf_op jit(solution)/shard_map/dot_general | solution.py:138
  165.7 3.1 copy.66
  169.8 1.6 subtract_convert_fusion
  172.3 1.5 collective-permute-start.2
  173.8 1.6 fusion.64
  175.4 7.0 %select_reduce_fusion.2 = (f32[256,5]{0,1:T(8,128)S(1)}, f32[256,5]{0,1:T(8,128)S(1)}, f32[256,5,2048]{2,0,1:T(8,128)}) fusion(pred[256,2048]{1,0:T(8,128)(4,1)S(1)} %iota_compare_fusion, f32[256,5,2048]{2,0,1:T(8,128)S(1)} %fusion.64, bf16[256,5,128]{0,2,1:T(8,128)(2,1)S(1)} %bitcast.101, bf16[2,2048,256]{2,1,0:T(8,128)(2,1)S(1)} %copy-done, s32[]{:T(128)S(6)} %select_n.135), kind=kOutput, calls=%fused_computation.5 | convolution fusion | flops 686814720 | bytes 22358020 | tf_op jit(solution)/shard_map/lge,ce->lgc/dot_general | solution.py:45
  185.5 5.5 %fusion.61 = f32[256,5,2048]{2,0,1:T(8,128)} fusion(bf16[256,5,128]{0,2,1:T(8,128)(2,1)S(1)} %bitcast.104, bf16[2,2048,256]{2,1,0:T(8,128)(2,1)S(1)} %copy-done, s32[]{:T(128)S(6)} %select_n.143), kind=kOutput, calls=%fused_computation.71 | convolution fusion | flops 671088640 | bytes 11337732 | tf_op jit(solution)/shard_map/lge,ce->lgc/dot_general | solution.py:45
  191.0 17.7 %fusion.2 = (f32[256,5]{0,1:T(8,128)S(1)}, f32[256,5]{0,1:T(8,128)S(1)}, f32[256,5]{0,1:T(8,128)S(1)}, f32[256,5]{0,1:T(8,128)S(1)}, f32[256,5,2048]{2,0,1:T(8,128)}) fusion(f32[256,5,2048]{2,0,1:T(8,128)} %get-tuple-element.57, f32[256,5]{0,1:T(8,128)S(1)} %get-tuple-element.50, pred[256,2048]{1,0:T(8,128)(4,1)S(1)} %iota_compare_fusion, ...), kind=kOutput, calls=%fused_computation.10 | convolution fusion | flops 707783680 | bytes 43356168 | tf_op jit(solution)/shard_map/lge,ce->lgc/dot_general | solution.py:45
  209.8 10.8 %fusion.4 = (f32[256,5]{0,1:T(8,128)S(1)}, f32[256,5]{0,1:T(8,128)S(1)}) fusion(f32[256,5,2048]{2,0,1:T(8,128)} %get-tuple-element.58, f32[256,5]{0,1:T(8,128)S(1)} %get-tuple-element.48, pred[256,2048]{1,0:T(8,128)(4,1)S(1)} %iota_compare_fusion, f32[256,5]{0,1:T(8,128)S(1)} %get-tuple-element.47, f32[256,5,2048]{2,0,1:T(8,128)} %fusion.61), kind=kLoop, calls=%fused_computation.12 | loop fusion | flops 20968960 | bytes 21516288 | tf_op jit(solution)/shard_map/reduce_sum | solution.py:56
  220.7 2.7 fusion.17
  223.7 2.7 fusion.51
  226.4 6.7 %fusion.48 = bf16[256,5,128]{0,2,1:T(8,128)(2,1)S(1)} fusion(bf16[256,5,128]{0,2,1:T(8,128)(2,1)S(1)} %fusion.51, f32[256,5,2048]{2,0,1:T(8,128)} %get-tuple-element.57, f32[256,5]{0,1:T(8,128)S(1)} %get-tuple-element.50, pred[256,2048]{1,0:T(8,128)(4,1)S(1)} %iota_compare_fusion, bf16[2,2048,256]{2,1,0:T(8,128)(2,1)S(1)} %copy-done.9, s32[]{:T(128)S(6)} %select_n.135, ...), kind=kOutput, calls=%fused_computation.54 | convolution fusion | flops 682393600 | bytes 12346372 | tf_op jit(solution)/shard_map/lgc,ce->lge/dot_general | solution.py:60
  233.1 2.7 select_convert_fusion
  236.1 1.5 collective-permute-start.3
  237.8 17.5 %all-gather.5.cloned.1.call-done = bf16[2560,1280]{1,0:T(8,128)(2,1)} async-done(((bf16[320,1280]{1,0:T(8,128)(2,1)}), bf16[2560,1280]{1,0:T(8,128)(2,1)}) %all-gather.5.cloned.1.call-update) | async-done | bytes 6553616 | tf_op jit(solution)/shard_map/all_gather | solution.py:193
  255.3 6.5 %fusion.56 = f32[256,2560]{1,0:T(8,128)} fusion(bf16[2560,1280]{1,0:T(8,128)(2,1)} %all-gather.5.cloned.1.call-done, s32[]{:T(128)S(6)} %select_n.158, bf16[1,256,1280]{1,2,0:T(8,128)(2,1)S(1)} %maximum_select_fusion, bf16[1,256,1280]{1,2,0:T(8,128)(2,1)S(1)} %bitcast.121), kind=kOutput, calls=%fused_computation.61 | convolution fusion | flops 1678049280 | bytes 10485764 | tf_op jit(solution)/shard_map/dot_general | solution.py:198
  261.9 5.2 %collective-permute-done.4 = f32[256,2560]{1,0:T(8,128)} collective-permute-done((f32[256,2560]{1,0:T(8,128)}, f32[256,2560]{1,0:T(8,128)}, u32[]{:S(2)}, u32[]{:S(2)}) %collective-permute-start.4) | collective-permute-done | bytes 2621472 | tf_op jit(solution)/shard_map/ppermute | solution.py:204
  267.1 5.8 %fusion.27 = bf16[256,2560]{1,0:T(8,128)(2,1)S(1)} fusion(f32[256,2560]{1,0:T(8,128)} %collective-permute-done.4, bf16[2560,1280]{1,0:T(8,128)(2,1)} %all-gather.5.cloned.1.call-done, s32[]{:T(128)S(6)} %select_n.153, bf16[1,256,1280]{1,2,0:T(8,128)(2,1)S(1)} %maximum_select_fusion, bf16[1,256,1280]{1,2,0:T(8,128)(2,1)} %bitcast.122), kind=kOutput, calls=%fused_computation.34 | convolution fusion | flops 1679360000 | bytes 11796484 | tf_op jit(solution)/shard_map/dot_general | solution.py:198
  273.0 1.5 collective-permute-start.5
  274.5 29.6 %collective-permute-done.5 = bf16[256,2560]{1,0:T(8,128)(2,1)} collective-permute-done((bf16[256,2560]{1,0:T(8,128)(2,1)S(1)}, bf16[256,2560]{1,0:T(8,128)(2,1)}, u32[]{:S(2)}, u32[]{:S(2)}) %collective-permute-start.5) | collective-permute-done | bytes 1310752 | tf_op jit(solution)/shard_map/ppermute | solution.py:99
  305.2 2.7 collective-permute-done.6
  309.1 1.4 fusion.99
  310.6 5.7 %concatenate.71 = bf16[256,5120]{1,0:T(8,128)(2,1)} concatenate(bf16[256,320]{1,0:T(8,128)(2,1)} %get-tuple-element.32, bf16[256,320]{1,0:T(8,128)(2,1)} %get-tuple-element.24, bf16[256,320]{1,0:T(8,128)(2,1)} %get-tuple-element.31, bf16[256,320]{1,0:T(8,128)(2,1)S(1)} %get-tuple-element.23, bf16[256,320]{1,0:T(8,128)(2,1)} %get-tuple-element.30, ...), dimensions={1} | concatenate | bytes 5242880 | tf_op jit(solution)/shard_map/concatenate | solution.py:216
  (110 shorter events, 16.6 us)
Async XLA Ops:
  6.5 167.2 %copy-start = (bf16[2,2048,256]{2,1,0:T(8,128)(2,1)S(1)}, bf16[2,2048,256]{2,1,0:T(8,128)(2,1)}, u32[]{:S(2)}) copy-start(bf16[2,2048,256]{2,1,0:T(8,128)(2,1)} %param.30) | copy-start | bytes 6291460
  6.5 146.1 %all-gather.3.cloned.1.call-start = ((), (), s32[]{:S(2)}) async-start(), calls=%async_computation | async-start | bytes 10321920 | tf_op jit(solution)/shard_map/all_gather | solution.py:137
  6.5 8.9 %copy-start.4 = (bf16[5120]{0:T(1024)(128)(2,1)S(1)}, bf16[5120]{0:T(1024)(128)(2,1)}, u32[]{:S(2)}) copy-start(bf16[5120]{0:T(1024)(128)(2,1)} %param.18) | copy-start | bytes 30724
  14.1 10.6 %copy-start.6 = (s32[256]{0:T(256)S(1)}, s32[256]{0:T(256)}, u32[]{:S(2)}) copy-start(s32[256]{0:T(256)} %param.33) | copy-start | bytes 3076
  14.2 10.6 %copy-start.5 = (f32[10,40]{1,0:T(8,128)S(1)}, f32[10,40]{1,0:T(8,128)}, u32[]{:S(2)}) copy-start(f32[10,40]{1,0:T(8,128)} %param.26) | copy-start | bytes 4804
  15.3 240.0 %all-gather.5.cloned.1.call-start = ((), (), s32[]{:S(2)}) async-start(), calls=%async_computation.1 | async-start | bytes 7372800 | tf_op jit(solution)/shard_map/all_gather | solution.py:193
  17.8 11.2 %copy-start.7 = (bf16[1280]{0:T(1024)(128)(2,1)S(1)}, bf16[1280]{0:T(1024)(128)(2,1)}, u32[]{:S(2)}) copy-start(bf16[1280]{0:T(1024)(128)(2,1)} %param.27) | copy-start | bytes 7684
  17.8 11.3 %copy-start.11 = (bf16[256]{0:T(256)(128)(2,1)S(1)}, bf16[256]{0:T(256)(128)(2,1)}, u32[]{:S(2)}) copy-start(bf16[256]{0:T(256)(128)(2,1)} %param.28) | copy-start | bytes 1540
  17.8 11.3 %copy-start.12 = (bf16[256]{0:T(256)(128)(2,1)S(1)}, bf16[256]{0:T(256)(128)(2,1)}, u32[]{:S(2)}) copy-start(bf16[256]{0:T(256)(128)(2,1)} %param.29) | copy-start | bytes 1540
  17.8 11.4 %copy-start.8 = (s32[256]{0:T(256)S(1)}, s32[256]{0:T(256)}, u32[]{:S(2)}) copy-start(s32[256]{0:T(256)} %param.32) | copy-start | bytes 3076
  21.8 60.7 %collective-permute-start = (bf16[256,5120]{1,0:T(8,128)(2,1)}, bf16[256,5120]{1,0:T(8,128)(2,1)}, u32[]{:S(2)}, u32[]{:S(2)}) collective-permute-start(bf16[256,5120]{1,0:T(8,128)(2,1)} %fusion.10), channel_id=1, source_target_pairs={{0,16},{16,0},{1,17},{17,1},{2,18},{18,2},{3,19},{19,3},{4,20},{20... | collective-permute-start | bytes 7864328 | tf_op jit(solution)/shard_map/ppermute | solution.py:99
  24.8 57.2 %collective-permute-start.1 = (s32[256]{0:T(256)S(1)}, s32[256]{0:T(256)S(1)}, u32[]{:S(2)}, u32[]{:S(2)}) collective-permute-start(s32[256]{0:T(256)S(1)} %copy-done.6), channel_id=1, source_target_pairs={{0,16},{16,0},{1,17},{17,1},{2,18},{18,2},{3,19},{19,3},{4,20},{20... | collective-permute-start | bytes 3080 | tf_op jit(solution)/shard_map/ppermute | solution.py:99
  172.3 12.2 %collective-permute-start.2 = (bf16[256,896]{0,1:T(8,128)(2,1)}, bf16[256,896]{0,1:T(8,128)(2,1)}, u32[]{:S(2)}, u32[]{:S(2)}) collective-permute-start(bf16[256,896]{0,1:T(8,128)(2,1)} %pad_maximum_fusion.2), channel_id=1, source_target_pairs={{0,16},{16,0},{1,17},{17,1},{2,18},{18,2},{3,19},{19,3},{4,20},{20... | collective-permute-start | bytes 1376264 | tf_op jit(solution)/shard_map/ppermute | solution.py:99
  175.3 7.3 %copy-start.2 = (f32[256,5,2048]{2,0,1:T(8,128)}, f32[256,5,2048]{2,0,1:T(8,128)S(1)}, u32[]{:S(2)}) copy-start(f32[256,5,2048]{2,0,1:T(8,128)S(1)} %fusion.64) | copy-start | bytes 31457284
  209.7 10.9 %copy-start.3 = (f32[256,5,2048]{2,0,1:T(8,128)S(1)}, f32[256,5,2048]{2,0,1:T(8,128)}, u32[]{:S(2)}) copy-start(f32[256,5,2048]{2,0,1:T(8,128)} %get-tuple-element.58) | copy-start | bytes 31457284
  209.7 10.9 %copy-start.9 = (bf16[2,2048,256]{2,1,0:T(8,128)(2,1)S(1)}, bf16[2,2048,256]{2,1,0:T(8,128)(2,1)}, u32[]{:S(2)}) copy-start(bf16[2,2048,256]{2,1,0:T(8,128)(2,1)} %param.31) | copy-start | bytes 6291460
  209.7 13.6 %slice-start = ((s8[10485760]{0:T(1024)(128)(4,1)}), s8[4194304]{0:T(1024)(128)(4,1)S(1)}, s32[]{:S(2)}) async-start(s8[10485760]{0:T(1024)(128)(4,1)} %bitcast.96), calls=%async_computation.2 | async-start | bytes 8388608
  209.7 13.6 %slice-start.1 = ((s8[10485760]{0:T(1024)(128)(4,1)}), s8[4194304]{0:T(1024)(128)(4,1)S(1)}, s32[]{:S(2)}) async-start(s8[10485760]{0:T(1024)(128)(4,1)} %bitcast.96), calls=%async_computation.3 | async-start | bytes 8388608
  220.6 3.1 slice-start.2
  223.7 9.4 %slice-start.3 = ((s8[10485760]{0:T(1024)(128)(4,1)}), s8[4194304]{0:T(1024)(128)(4,1)S(1)}, s32[]{:S(2)}) async-start(s8[10485760]{0:T(1024)(128)(4,1)} %bitcast.98), calls=%async_computation.5 | async-start | bytes 8388608
  223.7 9.4 %slice-start.4 = ((s8[10485760]{0:T(1024)(128)(4,1)}), s8[2097152]{0:T(1024)(128)(4,1)S(1)}, s32[]{:S(2)}) async-start(s8[10485760]{0:T(1024)(128)(4,1)} %bitcast.98), calls=%async_computation.6 | async-start | bytes 4194304
  226.4 6.7 %slice-start.5 = ((s8[10485760]{0:T(1024)(128)(4,1)}), s8[4194304]{0:T(1024)(128)(4,1)S(1)}, s32[]{:S(2)}) async-start(s8[10485760]{0:T(1024)(128)(4,1)} %bitcast.98), calls=%async_computation.7 | async-start | bytes 8388608
  236.1 19.2 %collective-permute-start.3 = (bf16[256,1280]{0,1:T(8,128)(2,1)S(1)}, bf16[256,1280]{0,1:T(8,128)(2,1)S(1)}, u32[]{:S(2)}, u32[]{:S(2)}) collective-permute-start(bf16[256,1280]{0,1:T(8,128)(2,1)S(1)} %maximum_select_fusion.1), channel_id=1, source_target_pairs={{0,16},{16,0},{1,17},{17,1},{2,18},{18,2},{3,19},{19,3},{4,20},{20... | collective-permute-start | bytes 1966088 | tf_op jit(solution)/shard_map/ppermute | solution.py:99
  255.3 6.5 %copy-start.10 = (bf16[256,1280]{0,1:T(8,128)(2,1)}, bf16[256,1280]{0,1:T(8,128)(2,1)S(1)}, u32[]{:S(2)}) copy-start(bf16[256,1280]{0,1:T(8,128)(2,1)S(1)} %collective-permute-done.3) | copy-start | bytes 1966084
  261.9 5.3 %collective-permute-start.4 = (f32[256,2560]{1,0:T(8,128)}, f32[256,2560]{1,0:T(8,128)}, u32[]{:S(2)}, u32[]{:S(2)}) collective-permute-start(f32[256,2560]{1,0:T(8,128)} %fusion.56), channel_id=1, source_target_pairs={{0,1},{1,0},{2,3},{3,2},{4,5},{5,4},{6,7},{7,6},{8,9},{9,8},{10,11... | collective-permute-start | bytes 7864328 | tf_op jit(solution)/shard_map/ppermute | solution.py:204
  273.0 31.2 %collective-permute-start.5 = (bf16[256,2560]{1,0:T(8,128)(2,1)S(1)}, bf16[256,2560]{1,0:T(8,128)(2,1)}, u32[]{:S(2)}, u32[]{:S(2)}) collective-permute-start(bf16[256,2560]{1,0:T(8,128)(2,1)S(1)} %fusion.27), channel_id=1, source_target_pairs={{0,16},{16,0},{1,17},{17,1},{2,18},{18,2},{3,19},{19,3},{4,20},{20... | collective-permute-start | bytes 3932168 | tf_op jit(solution)/shard_map/ppermute | solution.py:99
  304.3 3.6 %collective-permute-start.6 = (bf16[256,2560]{1,0:T(8,128)(2,1)S(1)}, bf16[256,2560]{1,0:T(8,128)(2,1)S(1)}, u32[]{:S(2)}, u32[]{:S(2)}) collective-permute-start(bf16[256,2560]{1,0:T(8,128)(2,1)S(1)} %broadcast_select_fusion), channel_id=1, source_target_pairs={{0,1},{1,0},{2,3},{3,2},{4,5},{5,4},{6,7},{7,6},{8,9},{9,8},{10,11... | collective-permute-start | bytes 3932168 | tf_op jit(solution)/shard_map/ppermute | solution.py:208
  308.0 8.2 %copy-start.1 = (bf16[2,2048,256]{2,1,0:T(8,128)(2,1)S(1)}, bf16[2,2048,256]{2,1,0:T(8,128)(2,1)}, u32[]{:S(2)}) copy-start(bf16[2,2048,256]{2,1,0:T(8,128)(2,1)} %param.30) | copy-start | bytes 6291460
Sparse Core Ops, SparseCore 0:
  15.5 137.1 all-gather.2
  154.9 100.4 all-gather.4
